TPU v7x, 32 devices: a whole 2x2x4 slice. The times are simulated.
32 devices in a mesh: rx: 4 (over z), ry: 8 (over y, x, core).
Axes of the slice: x: 2, y: 2, z: 4, core: 2. Of those that a mesh axis runs over, the one named last changes fastest.
Arguments:
- features: bfloat16 [256, 64, 512], P(('rx', 'ry')), may hold values from -6 to 6
- grad_out: bfloat16 [256, 64, 512], P(('rx', 'ry')), may hold values from -6 to 6
- weights: bfloat16 [27, 64, 64], replicated, may hold values from -0.15625 to 0.15625
- live_count: int32 [32], P(('rx', 'ry')), may hold values from 0 to 8, as said below
- neighbor: int32 [256, 6], P(('rx', 'ry')), may hold values from -1 to 23, as said below
- send_list: int32 [128, 4], P(('rx', 'ry')), may hold values from -1 to 7, as said below
Outputs:
- output: bfloat16 [256, 64, 512], P(('rx', 'ry'))
- grad_features: bfloat16 [256, 64, 512], P(('rx', 'ry'))
- grad_weights: float32 [27, 64, 64], replicated
Inputs may be any that keep to these rules, and one draw needn't show every extreme that they name: A device's occupied bricks take its first live_count slots; some device is full. `neighbor`: only live slots have entries other than -1. Entries of 8 or more stand only in columns 0 to 3, equal 8 + s * 4 + k in column s, and never point beyond the grid of devices. Sides 4 and 5 are always within the device. Adjacency is mutual: a brick is its neighbour's neighbour on the opposite side, and each received face slot of a side is used by at most one brick. `send_list`: row 4 d + t lists distinct live slots of device d, their face t going to the device beside d on side t; used entries come first, then -1.
All inputs are finite; a program needn't handle non-finite values.
Results may differ from a plain program's by a relative error of at most 0.0025.
Values may be sent and summed in bfloat16 or wider, within the bound.
A program may use at most 64 MiB of HBM per device.

v0:
```python
import functools

import jax
import jax.numpy as jnp
from jax import lax
from jax.experimental import pallas as pl
from jax.experimental.pallas import tpu as pltpu
from jax.sharding import PartitionSpec as P

MESH = pl.DeviceIdType.MESH
ROWS = 1024


def low_lanes(shape):
    return lax.broadcasted_iota(jnp.int32, shape, len(shape) - 1) < 64


def pack_kernel(live_ref, send_ref, feat_ref, grad_ref, t_ref, out_ref):
    slots = feat_ref.shape[0]

    def one(g, carry):
        both = jnp.concatenate([feat_ref[g], grad_ref[g]], axis=0).astype(jnp.float32)
        cells = jnp.transpose(both)
        cells = jnp.where(g < live_ref[0], cells, 0.0)
        t_ref[g] = cells.reshape(8, 8, 8, 128)
        return carry

    lax.fori_loop(0, slots, one, 0)
    for t in range(4):
        for k in range(send_ref.shape[1]):
            slot = send_ref[t, k]
            e = jnp.maximum(slot, 0)
            if t < 2:
                face = t_ref[e, 0 if t == 0 else 7]
            else:
                face = t_ref[e, :, 0 if t == 2 else 7]
            face = jnp.where(slot >= 0, face, 0.0)
            out_ref[t, k] = face.reshape(64, 128).astype(jnp.bfloat16)


def swap_kernel(n_rx, n_ry, send_ref, recv_ref, send_sem, recv_sem):
    row, col = lax.axis_index("rx"), lax.axis_index("ry")
    sides = [
        (row > 0, (row - 1, col)),
        (row < n_rx - 1, (row + 1, col)),
        (col > 0, (row, col - 1)),
        (col < n_ry - 1, (row, col + 1)),
    ]
    barrier = pltpu.get_barrier_semaphore()
    for there, peer in sides:

        @pl.when(there)
        def _():
            pl.semaphore_signal(barrier, inc=1, device_id=peer, device_id_type=MESH)

    peers = sum(jnp.where(there, 1, 0) for there, _ in sides)
    pl.semaphore_wait(barrier, peers)

    def copy(t, peer):
        return pltpu.make_async_remote_copy(
            src_ref=send_ref.at[t],
            dst_ref=recv_ref.at[t ^ 1],
            send_sem=send_sem.at[t],
            recv_sem=recv_sem.at[t ^ 1],
            device_id=peer,
            device_id_type=MESH,
        )

    def arrival(t, peer):
        return pltpu.make_async_remote_copy(
            src_ref=send_ref.at[t],
            dst_ref=recv_ref.at[t],
            send_sem=send_sem.at[t],
            recv_sem=recv_sem.at[t],
            device_id=peer,
            device_id_type=MESH,
        )

    for t, (there, peer) in enumerate(sides):

        @pl.when(there)
        def _():
            copy(t, peer).start()

        @pl.when(jnp.logical_not(there))
        def _():
            recv_ref[t] = jnp.zeros(recv_ref.shape[1:], recv_ref.dtype)

    for t, (there, peer) in enumerate(sides):

        @pl.when(there)
        def _():
            copy(t, peer).wait_send()
            arrival(t, peer).wait_recv()


def conv_kernel(
    slots, nb_ref, live_ref, t_ref, recv_ref, wf_ref, wb_ref,
    out_ref, gf_ref, dw_ref, pad, under, over, xs, acc,
):
    g = pl.program_id(0)
    cap = recv_ref.shape[1]

    @pl.when(g == 0)
    def _():
        pad[...] = jnp.zeros_like(pad)
        under[...] = jnp.zeros_like(under)
        over[...] = jnp.zeros_like(over)
        acc[...] = jnp.zeros_like(acc)

    own = t_ref[g]
    pad[1:9, 1:9] = own
    for s in range(4):
        entry = nb_ref[g, s]
        e = jnp.clip(entry, 0, slots - 1)
        k = jnp.maximum(entry - slots, 0) % cap
        layer = 7 if s % 2 == 0 else 0
        local = t_ref[e, layer] if s < 2 else t_ref[e, :, layer]
        far = recv_ref[s, k].astype(jnp.float32).reshape(8, 8, 128)
        face = jnp.where(entry >= slots, far, jnp.where(entry >= 0, local, 0.0))
        if s < 2:
            pad[9 * (s % 2), 1:9] = face
        else:
            pad[1:9, 9 * (s % 2)] = face
    for s, hold in ((4, under), (5, over)):
        entry = nb_ref[g, s]
        e = jnp.clip(entry, 0, slots - 1)
        hold[1:9, 1:9] = jnp.where(entry >= 0, t_ref[e], 0.0)

    mid = pad[...].reshape(100, 8, 128)
    level = lax.broadcasted_iota(jnp.int32, mid.shape, 1)
    low = pltpu.roll(jnp.where(level == 7, under[...].reshape(mid.shape), mid), 1, 1)
    high = pltpu.roll(jnp.where(level == 0, over[...].reshape(mid.shape), mid), 7, 1)
    mid, low, high = (v.reshape(800, 128) for v in (mid, low, high))
    first = low_lanes((800, 128))
    xs[:, 0:128] = jnp.where(first, low, pltpu.roll(mid, 64, 1)).astype(jnp.bfloat16)
    xs[:, 128:256] = high.astype(jnp.bfloat16)
    xs[:, 256:384] = jnp.where(first, pltpu.roll(low, 64, 1), mid).astype(jnp.bfloat16)

    yf = jnp.dot(xs[0:640, 0:256], wf_ref[0], preferred_element_type=jnp.float32)
    yb = jnp.dot(xs[0:640, 128:384], wb_ref[0], preferred_element_type=jnp.float32)
    for a in (1, 2):
        yf += jnp.dot(
            xs[80 * a : 80 * a + 640, 0:256], wf_ref[a], preferred_element_type=jnp.float32
        )
        yb += jnp.dot(
            xs[80 * a : 80 * a + 640, 128:384], wb_ref[a], preferred_element_type=jnp.float32
        )
    yf, yb = yf.reshape(8, 10, 8, 256), yb.reshape(8, 10, 8, 256)
    half = low_lanes((8, 8, 8, 128))
    swapped = jnp.where(half, yb[:, 1:9, :, 0:128], yf[:, 1:9, :, 0:128])
    total = jnp.where(half, yf[:, 0:8, :, 0:128], yb[:, 0:8, :, 0:128])
    total += yf[:, 2:10, :, 128:256] + yb[:, 2:10, :, 128:256]
    total = total.reshape(512, 128) + pltpu.roll(swapped.reshape(512, 128), 64, 1)
    total = jnp.where(g < live_ref[0], total, 0.0)
    flat = jnp.transpose(total).astype(jnp.bfloat16)
    out_ref[0] = flat[0:64]
    gf_ref[0] = flat[64:128]

    turned = pltpu.roll(own.reshape(512, 128), 64, 1).reshape(8, 8, 8, 128)
    zero = jnp.zeros((8, 1, 8, 128), jnp.float32)
    g0 = jnp.concatenate([turned, zero, zero], axis=1)
    g1 = jnp.concatenate([zero, own, zero], axis=1)
    g2 = jnp.concatenate([zero, zero, turned], axis=1)
    g01 = jnp.where(low_lanes(g0.shape), g0, g1)
    lhs = jnp.concatenate(
        [jnp.transpose(g01.reshape(640, 128)), jnp.transpose(g2.reshape(640, 128))[0:64]], axis=0
    ).astype(jnp.bfloat16)
    for a in range(3):
        acc[192 * a : 192 * a + 192] += jnp.dot(
            lhs, xs[80 * a : 80 * a + 640, 0:256], preferred_element_type=jnp.float32
        )

    @pl.when(g == slots - 1)
    def _():
        dw_ref[0:576] = acc[:, 0:128]
        top, rest = acc[0:288, 128:256], acc[288:576, 128:256]
        dw_ref[576:864] = jnp.where(low_lanes((288, 128)), top, pltpu.roll(rest, 64, 1))
        dw_ref[864:ROWS] = jnp.zeros((ROWS - 864, 128), jnp.float32)


def sum_kernel(
    n_rx, n_ry, scale, dw_ref, out_ref,
    src1, got1, src2, got2, part, whole, send_sem, sem1, sem2, sem3, sem4,
):
    row, col = lax.axis_index("rx"), lax.axis_index("ry")
    size = dw_ref.shape[0] // n_ry
    piece = size // n_rx
    cols = [lax.rem(col + d, n_ry) for d in range(1, n_ry)]
    rows = [lax.rem(row + d, n_rx) for d in range(1, n_rx)]
    barrier = pltpu.get_barrier_semaphore()
    for c in cols:
        pl.semaphore_signal(barrier, inc=1, device_id=(row, c), device_id_type=MESH)
    for r in rows:
        pl.semaphore_signal(barrier, inc=1, device_id=(r, col), device_id_type=MESH)
    src1[...] = dw_ref[...].reshape(n_ry, size, 128)
    pl.semaphore_wait(barrier, n_ry + n_rx - 2)

    def copy(src, dst, stage, n, sem, peer):
        return pltpu.make_async_remote_copy(
            src_ref=src, dst_ref=dst, send_sem=send_sem.at[stage, n], recv_sem=sem,
            device_id=peer, device_id_type=MESH,
        )

    sent = []
    for n, c in enumerate(cols):
        x = copy(src1.at[c], got1.at[col], 0, n, sem1.at[col], (row, c))
        x.start()
        sent.append(x)
    mine = dw_ref[pl.ds(pl.multiple_of(col * size, 8), size), :]
    for n, c in enumerate(reversed(cols)):
        copy(src1.at[c], got1.at[c], 0, n, sem1.at[c], (row, c)).wait_recv()
        mine += got1[c]

    src2[...] = mine.reshape(n_rx, piece, 128)
    for n, r in enumerate(rows):
        x = copy(src2.at[r], got2.at[row], 1, n, sem2.at[row], (r, col))
        x.start()
        sent.append(x)
    small = src2[row]
    for n, r in enumerate(reversed(rows)):
        copy(src2.at[r], got2.at[r], 1, n, sem2.at[r], (r, col)).wait_recv()
        small += got2[r]

    part[row] = (small * scale).astype(part.dtype)
    for n, r in enumerate(rows):
        x = copy(part.at[row], part.at[row], 2, n, sem3.at[row], (r, col))
        x.start()
        sent.append(x)
    for n, r in enumerate(reversed(rows)):
        copy(part.at[r], part.at[r], 2, n, sem3.at[r], (r, col)).wait_recv()

    for n, c in enumerate(cols):
        x = copy(part, whole.at[col], 3, n, sem4.at[col], (row, c))
        x.start()
        sent.append(x)
    out_ref[col] = part[...].astype(jnp.float32)
    for n, c in enumerate(reversed(cols)):
        copy(part, whole.at[c], 3, n, sem4.at[c], (row, c)).wait_recv()
        out_ref[c] = whole[c].astype(jnp.float32)
    for x in sent:
        x.wait_send()


def body(features, grad_out, weights, live_count, neighbor, send_list):
    slots, channels = features.shape[0], features.shape[1]
    cap = send_list.shape[1]
    n_rx, n_ry = lax.axis_size("rx"), lax.axis_size("ry")
    f32, bf16 = jnp.float32, jnp.bfloat16
    vmem = pl.BlockSpec(memory_space=pltpu.VMEM)
    smem = pl.BlockSpec(memory_space=pltpu.SMEM)

    cells, faces = pl.pallas_call(
        pack_kernel,
        out_shape=(
            jax.ShapeDtypeStruct((slots, 8, 8, 8, 128), f32),
            jax.ShapeDtypeStruct((4, cap, 64, 128), bf16),
        ),
        in_specs=[smem, smem, vmem, vmem],
        out_specs=(vmem, vmem),
        name="pack",
    )(live_count, send_list, features, grad_out)

    received = pl.pallas_call(
        functools.partial(swap_kernel, n_rx, n_ry),
        out_shape=jax.ShapeDtypeStruct((4, cap, 64, 128), bf16),
        in_specs=[vmem],
        out_specs=vmem,
        scratch_shapes=[pltpu.SemaphoreType.DMA((4,)), pltpu.SemaphoreType.DMA((4,))],
        compiler_params=pltpu.CompilerParams(collective_id=0, has_side_effects=True),
        name="swap",
    )(faces)

    by_offset = weights.reshape(3, 3, 3, channels, channels)
    forward = by_offset.transpose(0, 2, 4, 1, 3).reshape(3, 192, 192)
    forward = jnp.pad(forward, ((0, 0), (0, 64), (0, 64)))
    backward = by_offset[::-1, ::-1, ::-1].transpose(0, 2, 3, 1, 4)
    gap = jnp.zeros((3, 3, 64, 1, 64), bf16)
    backward = jnp.concatenate(
        [backward[:, :, :, 1:2], backward[:, :, :, 0:1], gap, backward[:, :, :, 2:3]], axis=3
    ).reshape(3, 3, 64, 256)
    backward = jnp.concatenate(
        [jnp.zeros((3, 64, 256), bf16), backward[:, 2], backward[:, 0], backward[:, 1]], axis=1
    )

    block = pl.BlockSpec((1, channels, 512), lambda g: (g, 0, 0))
    output, grad_features, dw = pl.pallas_call(
        functools.partial(conv_kernel, slots),
        grid=(slots,),
        out_shape=(
            jax.ShapeDtypeStruct(features.shape, bf16),
            jax.ShapeDtypeStruct(features.shape, bf16),
            jax.ShapeDtypeStruct((ROWS, 128), f32),
        ),
        in_specs=[smem, smem, vmem, vmem, vmem, vmem],
        out_specs=(block, block, pl.BlockSpec((ROWS, 128), lambda g: (0, 0))),
        scratch_shapes=[
            pltpu.VMEM((10, 10, 8, 128), f32),
            pltpu.VMEM((10, 10, 8, 128), f32),
            pltpu.VMEM((10, 10, 8, 128), f32),
            pltpu.VMEM((800, 384), bf16),
            pltpu.VMEM((576, 256), f32),
        ],
        name="conv",
    )(neighbor, live_count, cells, received, forward, backward)

    scale = (512.0 * slots * n_rx * n_ry) ** (-0.5)
    size = ROWS // n_ry
    piece = size // n_rx
    most = max(n_rx, n_ry)
    summed = pl.pallas_call(
        functools.partial(sum_kernel, n_rx, n_ry, scale),
        out_shape=jax.ShapeDtypeStruct((n_ry, n_rx, piece, 128), f32),
        in_specs=[vmem],
        out_specs=vmem,
        scratch_shapes=[
            pltpu.VMEM((n_ry, size, 128), f32),
            pltpu.VMEM((n_ry, size, 128), f32),
            pltpu.VMEM((n_rx, piece, 128), f32),
            pltpu.VMEM((n_rx, piece, 128), f32),
            pltpu.VMEM((n_rx, piece, 128), bf16),
            pltpu.VMEM((n_ry, n_rx, piece, 128), bf16),
            pltpu.SemaphoreType.DMA((4, most)),
            pltpu.SemaphoreType.DMA((n_ry,)),
            pltpu.SemaphoreType.DMA((n_rx,)),
            pltpu.SemaphoreType.DMA((n_rx,)),
            pltpu.SemaphoreType.DMA((n_ry,)),
        ],
        compiler_params=pltpu.CompilerParams(collective_id=1, has_side_effects=True),
        name="total",
    )(dw).reshape(ROWS, 128)
    pairs = summed[0:576].reshape(3, 3, 64, 2, 64)
    last = jnp.concatenate([summed[576:864, 0:64], summed[576:864, 64:128]], axis=0)
    joined = jnp.concatenate([pairs, last.reshape(3, 3, 64, 1, 64)], axis=3)
    grad_weights = joined.transpose(0, 1, 3, 2, 4).reshape(27, channels, channels)
    return output, grad_features, grad_weights


def solution(mesh):
    placed = (
        P(("rx", "ry"), None, None),
        P(("rx", "ry"), None, None),
        P(),
        P(("rx", "ry")),
        P(("rx", "ry"), None),
        P(("rx", "ry"), None),
    )
    return jax.shard_map(
        body,
        mesh=mesh,
        in_specs=placed,
        out_specs=(P(("rx", "ry"), None, None), P(("rx", "ry"), None, None), P()),
        check_vma=False,
    )
```

profile of v0, /device:TPU:0, one launch (start us, length us, event | category | flops | bytes accessed | tf_op | source)
XLA Modules:
  0.0 61.0 jit_solution(8458171149601005662)
XLA Ops:
  1.3 0.1 pad.15.clone
  1.4 1.4 %copy.14 = bf16[3,3,3,64,64]{4,1,3,0,2:T(4,128)(2,1)S(1)} copy(bf16[3,3,3,64,64]{4,3,2,1,0:T(8,128)(2,1)} %bitcast.23) | data formatting | bytes 442368 | tf_op jit(solution)/shard_map/reshape | solution.py:274
  2.8 1.6 %rev.3 = bf16[3,3,3,64,64]{4,1,3,0,2:T(4,128)(2,1)S(1)} reverse(bf16[3,3,3,64,64]{4,1,3,0,2:T(4,128)(2,1)S(1)} %copy.14), dimensions={0,1,2} | reverse | bytes 442368 | tf_op jit(solution)/shard_map/rev | solution.py:277
  4.4 0.9 %fusion = (bf16[3,3,64,1,64]{4,3,2,0,1:T(2,128)(2,1)S(1)}, bf16[3,3,64,1,64]{4,3,2,0,1:T(2,128)(2,1)S(1)}, bf16[3,3,64,1,64]{4,3,2,0,1:T(2,128)(2,1)S(1)}) fusion(bf16[3,3,64,3,64]{4,3,2,0,1:T(4,128)(2,1)S(1)} %bitcast.19), kind=kLoop, calls=%fused_computation.7 | loop fusion | bytes 442368 | tf_op jit(solution)/shard_map/slice | solution.py:280
  5.3 1.3 %pad_maximum_fusion.1 = bf16[3,3,64,4,64]{4,3,2,0,1:T(4,128)(2,1)S(1)} fusion(bf16[3,3,64,1,64]{4,3,2,0,1:T(2,128)(2,1)S(1)} %get-tuple-element.14, bf16[3,3,64,1,64]{4,3,2,0,1:T(2,128)(2,1)S(1)} %get-tuple-element.15, bf16[3,3,64,1,64]{4,3,2,0,1:T(2,128)(2,1)S(1)} %get-tuple-element.13, bf16[4]{0:T(256)(128)(2,1)S(1)} %pad.15.clone), kind=kLoop, calls=%fused_computation.1 | loop fusion | flops 1179648 | bytes 516104 | tf_op jit(solution)/shard_map/concatenate | solution.py:279
  6.6 0.0 copy-start
  6.6 0.4 reshape.29
  7.1 0.9 %pad_maximum_fusion.2.wb_ref = bf16[3,256,256]{2,1,0:T(8,128)(2,1)} fusion(bf16[3,64,256]{2,1,0:T(8,128)(2,1)S(1)} %get-tuple-element.19, bf16[3,64,256]{2,1,0:T(8,128)(2,1)S(1)} %get-tuple-element.20, bf16[3,64,256]{2,1,0:T(8,128)(2,1)S(1)} %get-tuple-element.18, bf16[256]{0:T(256)(128)(2,1)S(1)} %pad.9.clone), kind=kLoop, calls=%fused_computation.2 | loop fusion | flops 1572864 | bytes 688640 | tf_op jit(solution)/shard_map/concatenate | solution.py:282
  7.9 0.0 copy-done
  7.9 1.0 %copy.13 = bf16[3,3,3,64,64]{3,1,4,2,0:T(4,128)(2,1)S(1)} copy(bf16[3,3,3,64,64]{4,3,2,1,0:T(8,128)(2,1)S(1)} %bitcast.24) | data formatting | bytes 442368 | tf_op jit(solution)/shard_map/reshape | solution.py:274
  8.9 0.4 reshape.28
  9.2 0.8 %pad.4.wf_ref = bf16[3,256,256]{2,1,0:T(8,128)(2,1)} pad(bf16[3,192,192]{2,1,0:T(8,128)(2,1)S(1)} %reshape.28, bf16[]{:T(256)} %constant.1.clone.1), padding=0_0x0_64x0_64 | pad | bytes 614402 | tf_op jit(solution)/shard_map/jit(_pad)/pad | solution.py:276
  10.0 3.5 %pack.1 = (f32[8,8,8,8,128]{4,3,2,1,0:T(8,128)}, bf16[4,4,64,128]{3,2,1,0:T(8,128)(2,1)}) custom-call(s32[1]{0:T(128)S(6)} %copy.17.live_ref, s32[4,4]{1,0:T(4,128)} %send_ref.1, bf16[8,64,512]{2,1,0:T(8,128)(2,1)} %feat_ref.1, bf16[8,64,512]{2,1,0:T(8,128)(2,1)} %grad_ref.1), custom_call_target="tpu_custom_call" | custom-call | tf_op jit(solution)/shard_map/pack/pallas_call | solution.py:253
  13.5 8.6 %swap.1.recv_ref = bf16[4,4,64,128]{3,2,1,0:T(8,128)(2,1)} custom-call(bf16[4,4,64,128]{3,2,1,0:T(8,128)(2,1)} %get-tuple-element.9.send_ref), custom_call_target="tpu_custom_call" | custom-call | tf_op jit(solution)/shard_map/swap/pallas_call | solution.py:264
  22.2 11.4 %conv.1 = (bf16[8,64,512]{2,1,0:T(8,128)(2,1)}, bf16[8,64,512]{2,1,0:T(8,128)(2,1)}, f32[1024,128]{1,0:T(8,128)}) custom-call(s32[8,6]{1,0:T(8,128)} %nb_ref.1, s32[1]{0:T(128)S(6)} %copy.17.live_ref, f32[8,8,8,8,128]{4,3,2,1,0:T(8,128)} %get-tuple-element.8.t_ref, bf16[4,4,64,128]{3,2,1,0:T(8,128)(2,1)} %swap.1.recv_ref, bf16[3,256,256]{2,1,0:T(8,128)(2,1)} %pad.4.wf_ref, ...), custom_call_target="tpu_custom_call" | custom-call | tf_op jit(solution)/shard_map/conv/pallas_call | solution.py:287
  33.6 23.9 %total.1 = f32[8,4,32,128]{3,2,1,0:T(8,128)} custom-call(f32[1024,128]{1,0:T(8,128)} %get-tuple-element.12.dw_ref), custom_call_target="tpu_custom_call" | custom-call | tf_op jit(solution)/shard_map/total/pallas_call | solution.py:311
  57.5 1.0 %slice.42 = f32[576,128]{1,0:T(8,128)S(1)} slice(f32[1024,128]{1,0:T(8,128)} %bitcast.20), slice={[0:576], [0:128]} | slice | bytes 589824 | tf_op jit(solution)/shard_map/slice | solution.py:332
  58.5 1.1 %fusion.1 = (f32[288,64]{1,0:T(8,128)S(1)}, f32[288,64]{1,0:T(8,128)S(1)}) fusion(f32[1024,128]{1,0:T(8,128)} %bitcast.21), kind=kLoop, calls=%fused_computation.8 | loop fusion | bytes 294912 | tf_op jit(solution)/shard_map/slice | solution.py:333
  59.6 0.4 reshape.31
  60.0 0.1 copy.15
  60.0 1.0 %pad_maximum_fusion = f32[3,3,64,3,64]{4,2,3,1,0:T(8,128)} fusion(f32[3,3,64,1,64]{4,2,3,1,0:T(8,128)S(1)} %bitcast.25, f32[3,3,64,2,64]{4,2,3,1,0:T(8,128)S(1)} %copy.15), kind=kLoop, calls=%fused_computation | loop fusion | flops 110592 | bytes 884736 | tf_op jit(solution)/shard_map/concatenate | solution.py:334
  (4 shorter events, 0.1 us)
Async XLA Ops:
  6.6 1.3 %copy-start = (bf16[27,64,64]{2,1,0:T(8,128)(2,1)S(1)}, bf16[27,64,64]{2,1,0:T(8,128)(2,1)}, u32[]{:S(2)}) copy-start(bf16[27,64,64]{2,1,0:T(8,128)(2,1)} %param.8) | copy-start | bytes 663556
where the time goes:
time: 61.4 us; the launch traced here: 61 us
  Pallas kernels  47.5 us (77%)
  local copies, waits for them, and re-layouts  8.99 us (15%)
  other arithmetic  3.2 us (5%)
  between operations  1.39 us (2%)
    pallas_call x1, Pallas kernels, body(): pl.pallas_call(functools.partial(sum_kernel, n_rx, n_ry, scale), out_shap...  23.9 us
    pallas_call x1, Pallas kernels, body(): pl.pallas_call(functools.partial(conv_kernel, slots), grid=(slots,), out_...  11.4 us
    pallas_call x1, Pallas kernels, body(): pl.pallas_call(functools.partial(swap_kernel, n_rx, n_ry), out_shape=jax....  8.64 us
    pallas_call x1, Pallas kernels, body(): pl.pallas_call(pack_kernel, out_shape=(jax.ShapeDtypeStruct((slots, 8, 8,...  3.48 us
    reshape x2, local copies, waits for them, and re-layouts, body(): by_offset = weights.reshape(3, 3, 3, channels, channels)  2.35 us
    rev x1, local copies, waits for them, and re-layouts, body(): backward = by_offset[::-1, ::-1, ::-1].transpose(0, 2, 3, 1, 4)  1.64 us
    concatenate x1, other arithmetic, body(): jnp.concatenate([backward[:, :, :, 1:2], backward[:, :, :, 0:1], gap, bac...  1.3 us

commit v1 on v0

--- a/solution.py
+++ b/solution.py
@@ -38,7 +38,10 @@
             out_ref[t, k] = face.reshape(64, 128).astype(jnp.bfloat16)
 
 
-def swap_kernel(n_rx, n_ry, send_ref, recv_ref, send_sem, recv_sem):
+def swap_kernel(
+    n_rx, n_ry, live_ref, list_ref, feat_ref, grad_ref, w_ref,
+    t_ref, recv_ref, wf_ref, wb_ref, send_ref, send_sem, recv_sem,
+):
     row, col = lax.axis_index("rx"), lax.axis_index("ry")
     sides = [
         (row > 0, (row - 1, col)),
@@ -53,45 +56,50 @@
         def _():
             pl.semaphore_signal(barrier, inc=1, device_id=peer, device_id_type=MESH)
 
+    pack_kernel(live_ref, list_ref, feat_ref, grad_ref, t_ref, send_ref)
     peers = sum(jnp.where(there, 1, 0) for there, _ in sides)
     pl.semaphore_wait(barrier, peers)
 
-    def copy(t, peer):
+    def copy(t, into, peer):
         return pltpu.make_async_remote_copy(
             src_ref=send_ref.at[t],
-            dst_ref=recv_ref.at[t ^ 1],
+            dst_ref=recv_ref.at[into],
             send_sem=send_sem.at[t],
-            recv_sem=recv_sem.at[t ^ 1],
+            recv_sem=recv_sem.at[into],
             device_id=peer,
             device_id_type=MESH,
         )
 
-    def arrival(t, peer):
-        return pltpu.make_async_remote_copy(
-            src_ref=send_ref.at[t],
-            dst_ref=recv_ref.at[t],
-            send_sem=send_sem.at[t],
-            recv_sem=recv_sem.at[t],
-            device_id=peer,
-            device_id_type=MESH,
-        )
-
     for t, (there, peer) in enumerate(sides):
 
         @pl.when(there)
         def _():
-            copy(t, peer).start()
+            copy(t, t ^ 1, peer).start()
 
         @pl.when(jnp.logical_not(there))
         def _():
             recv_ref[t] = jnp.zeros(recv_ref.shape[1:], recv_ref.dtype)
 
+    gap = jnp.zeros((64, 64), jnp.float32)
+    wide = jnp.zeros((64, 256), jnp.bfloat16)
+    for a in range(3):
+        wf_ref[a, 192:256] = wide
+        wb_ref[a, 0:64] = wide
+        for c in range(3):
+            ahead = [w_ref[9 * a + 3 * b + c].astype(jnp.float32) for b in range(3)]
+            block = jnp.transpose(jnp.concatenate(ahead + [gap], axis=0))
+            wf_ref[a, 64 * c : 64 * c + 64] = block.astype(jnp.bfloat16)
+            back = [w_ref[26 - 9 * a - 3 * b - c].astype(jnp.float32) for b in range(3)]
+            block = jnp.concatenate([back[1], back[0], gap, back[2]], axis=1)
+            at = 64 * (2, 3, 1)[c]
+            wb_ref[a, at : at + 64] = block.astype(jnp.bfloat16)
+
     for t, (there, peer) in enumerate(sides):
 
         @pl.when(there)
         def _():
-            copy(t, peer).wait_send()
-            arrival(t, peer).wait_recv()
+            copy(t, t ^ 1, peer).wait_send()
+            copy(t, t, peer).wait_recv()
 
 
 def conv_kernel(
@@ -174,9 +182,10 @@
     @pl.when(g == slots - 1)
     def _():
         dw_ref[0:576] = acc[:, 0:128]
-        top, rest = acc[0:288, 128:256], acc[288:576, 128:256]
-        dw_ref[576:864] = jnp.where(low_lanes((288, 128)), top, pltpu.roll(rest, 64, 1))
-        dw_ref[864:ROWS] = jnp.zeros((ROWS - 864, 128), jnp.float32)
+        rest = jnp.concatenate([acc[320:576, 128:256], jnp.zeros((64, 128), jnp.float32)], axis=0)
+        top = acc[0:320, 128:256]
+        dw_ref[576:896] = jnp.where(low_lanes((320, 128)), top, pltpu.roll(rest, 64, 1))
+        dw_ref[896:ROWS] = jnp.zeros((ROWS - 896, 128), jnp.float32)
 
 
 def sum_kernel(
@@ -234,10 +243,16 @@
         x = copy(part, whole.at[col], 3, n, sem4.at[col], (row, c))
         x.start()
         sent.append(x)
-    out_ref[col] = part[...].astype(jnp.float32)
+    whole[col] = part[...]
     for n, c in enumerate(reversed(cols)):
         copy(part, whole.at[c], 3, n, sem4.at[c], (row, c)).wait_recv()
-        out_ref[c] = whole[c].astype(jnp.float32)
+    full = whole[...].astype(jnp.float32).reshape(ROWS, 128)
+    for n in range(9):
+        pair = full[64 * n : 64 * n + 64]
+        out_ref[3 * n] = pair[:, 0:64]
+        out_ref[3 * n + 1] = pair[:, 64:128]
+        at, half = 576 + 64 * (n % 5), 64 * (n // 5)
+        out_ref[3 * n + 2] = full[at : at + 64, half : half + 64]
     for x in sent:
         x.wait_send()
 
@@ -250,38 +265,24 @@
     vmem = pl.BlockSpec(memory_space=pltpu.VMEM)
     smem = pl.BlockSpec(memory_space=pltpu.SMEM)
 
-    cells, faces = pl.pallas_call(
-        pack_kernel,
+    cells, received, forward, backward = pl.pallas_call(
+        functools.partial(swap_kernel, n_rx, n_ry),
         out_shape=(
             jax.ShapeDtypeStruct((slots, 8, 8, 8, 128), f32),
             jax.ShapeDtypeStruct((4, cap, 64, 128), bf16),
+            jax.ShapeDtypeStruct((3, 256, 256), bf16),
+            jax.ShapeDtypeStruct((3, 256, 256), bf16),
         ),
-        in_specs=[smem, smem, vmem, vmem],
-        out_specs=(vmem, vmem),
-        name="pack",
-    )(live_count, send_list, features, grad_out)
-
-    received = pl.pallas_call(
-        functools.partial(swap_kernel, n_rx, n_ry),
-        out_shape=jax.ShapeDtypeStruct((4, cap, 64, 128), bf16),
-        in_specs=[vmem],
-        out_specs=vmem,
-        scratch_shapes=[pltpu.SemaphoreType.DMA((4,)), pltpu.SemaphoreType.DMA((4,))],
+        in_specs=[smem, smem, vmem, vmem, vmem],
+        out_specs=(vmem, vmem, vmem, vmem),
+        scratch_shapes=[
+            pltpu.VMEM((4, cap, 64, 128), bf16),
+            pltpu.SemaphoreType.DMA((4,)),
+            pltpu.SemaphoreType.DMA((4,)),
+        ],
         compiler_params=pltpu.CompilerParams(collective_id=0, has_side_effects=True),
         name="swap",
-    )(faces)
-
-    by_offset = weights.reshape(3, 3, 3, channels, channels)
-    forward = by_offset.transpose(0, 2, 4, 1, 3).reshape(3, 192, 192)
-    forward = jnp.pad(forward, ((0, 0), (0, 64), (0, 64)))
-    backward = by_offset[::-1, ::-1, ::-1].transpose(0, 2, 3, 1, 4)
-    gap = jnp.zeros((3, 3, 64, 1, 64), bf16)
-    backward = jnp.concatenate(
-        [backward[:, :, :, 1:2], backward[:, :, :, 0:1], gap, backward[:, :, :, 2:3]], axis=3
-    ).reshape(3, 3, 64, 256)
-    backward = jnp.concatenate(
-        [jnp.zeros((3, 64, 256), bf16), backward[:, 2], backward[:, 0], backward[:, 1]], axis=1
-    )
+    )(live_count, send_list, features, grad_out, weights)
 
     block = pl.BlockSpec((1, channels, 512), lambda g: (g, 0, 0))
     output, grad_features, dw = pl.pallas_call(
@@ -308,9 +309,9 @@
     size = ROWS // n_ry
     piece = size // n_rx
     most = max(n_rx, n_ry)
-    summed = pl.pallas_call(
+    grad_weights = pl.pallas_call(
         functools.partial(sum_kernel, n_rx, n_ry, scale),
-        out_shape=jax.ShapeDtypeStruct((n_ry, n_rx, piece, 128), f32),
+        out_shape=jax.ShapeDtypeStruct((27, channels, channels), f32),
         in_specs=[vmem],
         out_specs=vmem,
         scratch_shapes=[
@@ -328,11 +329,7 @@
         ],
         compiler_params=pltpu.CompilerParams(collective_id=1, has_side_effects=True),
         name="total",
-    )(dw).reshape(ROWS, 128)
-    pairs = summed[0:576].reshape(3, 3, 64, 2, 64)
-    last = jnp.concatenate([summed[576:864, 0:64], summed[576:864, 64:128]], axis=0)
-    joined = jnp.concatenate([pairs, last.reshape(3, 3, 64, 1, 64)], axis=3)
-    grad_weights = joined.transpose(0, 1, 3, 2, 4).reshape(27, channels, channels)
+    )(dw)
     return output, grad_features, grad_weights
 
 

time: 61.4 us -> 49.6 us (0.81)
  local copies, waits for them, and re-layouts: 8.99 us -> 2.17 us
  other arithmetic: 3.2 us -> 0 us
  Pallas kernels: 47.5 us -> 45.9 us
    reshape x6 -> x0, local copies, waits for them, and re-layouts: 3.48 us -> none  [the longest x2 2.35 us: body(): by_offset = weights.reshape(3, 3, 3, channels, channels)]
    concatenate x4 -> x0, other arithmetic: 3.2 us -> none  [the longest x1 1.3 us: body(): jnp.concatenate([backward[:, :, :, 1:2], backward[:, :, :, 0:1], gap, bac...]
    slice x3 -> x0, local copies, waits for them, and re-layouts: 2.97 us -> none  [the longest x1 1.08 us: body(): summed[576:864, 0:64]]
    unnamed x2 -> x1, local copies, waits for them, and re-layouts: 0.01 us -> 2.17 us
    pallas_call x2 -> x1, Pallas kernels: 12.1 us -> 10 us  [body(): pl.pallas_call(functools.partial(swap_kernel, n_rx, n_ry), out_shape=(jax...]
    rev x1 -> x0, local copies, waits for them, and re-layouts: 1.64 us -> none  [body(): backward = by_offset[::-1, ::-1, ::-1].transpose(0, 2, 3, 1, 4)]
    pad x1 -> x0, local copies, waits for them, and re-layouts: 0.78 us -> none  [body(): forward = jnp.pad(forward, ((0, 0), (0, 64), (0, 64)))]
where the time goes in v1:
time: 49.6 us; the launch traced here: 49.4 us
  Pallas kernels  45.9 us (93%)
  local copies, waits for them, and re-layouts  2.17 us (4%)
  between operations  1.3 us (3%)
    pallas_call x1, Pallas kernels, body(): pl.pallas_call(functools.partial(sum_kernel, n_rx, n_ry, scale), out_shap...  24.5 us
    pallas_call x1, Pallas kernels, body(): pl.pallas_call(functools.partial(conv_kernel, slots), grid=(slots,), out_...  11.4 us
    pallas_call x1, Pallas kernels, body(): pl.pallas_call(functools.partial(swap_kernel, n_rx, n_ry), out_shape=(jax...  10 us
    unnamed x1, local copies, waits for them, and re-layouts  2.17 us

profile of v1, /device:TPU:0, one launch (start us, length us, event | category | flops | bytes accessed | tf_op | source)
XLA Modules:
  0.0 49.4 jit_solution(15345307311408728014)
XLA Ops:
  1.3 10.0 %swap.1 = (f32[8,8,8,8,128]{4,3,2,1,0:T(8,128)}, bf16[4,4,64,128]{3,2,1,0:T(8,128)(2,1)}, bf16[3,256,256]{2,1,0:T(8,128)(2,1)}, bf16[3,256,256]{2,1,0:T(8,128)(2,1)}) custom-call(s32[1]{0:T(128)S(6)} %copy.10.live_ref, s32[4,4]{1,0:T(4,128)} %list_ref.1, bf16[8,64,512]{2,1,0:T(8,128)(2,1)} %feat_ref.1, bf16[8,64,512]{2,1,0:T(8,128)(2,1)} %grad_ref.1, ...), custom_call_target="tpu_custom_call" | custom-call | tf_op jit(solution)/shard_map/swap/pallas_call | solution.py:268
  11.3 11.4 %conv.1 = (bf16[8,64,512]{2,1,0:T(8,128)(2,1)}, bf16[8,64,512]{2,1,0:T(8,128)(2,1)}, f32[1024,128]{1,0:T(8,128)}) custom-call(s32[8,6]{1,0:T(8,128)} %nb_ref.1, s32[1]{0:T(128)S(6)} %copy.10.live_ref, f32[8,8,8,8,128]{4,3,2,1,0:T(8,128)} %get-tuple-element.10.t_ref, bf16[4,4,64,128]{3,2,1,0:T(8,128)(2,1)} %get-tuple-element.11.recv_ref, ...), custom_call_target="tpu_custom_call" | custom-call | tf_op jit(solution)/shard_map/conv/pallas_call | solution.py:288
  22.7 24.5 %total.1 = f32[27,64,64]{2,1,0:T(8,128)} custom-call(f32[1024,128]{1,0:T(8,128)} %get-tuple-element.16.dw_ref), custom_call_target="tpu_custom_call" | custom-call | tf_op jit(solution)/shard_map/total/pallas_call | solution.py:312
  47.2 2.2 %copy.11 = f32[27,64,64]{2,1,0:T(8,128)} copy(f32[27,64,64]{2,1,0:T(8,128)} %total.1) | data formatting | bytes 884736

commit v2 on v1

--- a/solution.py
+++ b/solution.py
@@ -102,10 +102,32 @@
             copy(t, t, peer).wait_recv()
 
 
+def apply_brick(g, live_ref, xs_ref, wf_ref, wb_ref, out_ref, gf_ref):
+    yf = jnp.dot(xs_ref[g, 0:640, 0:256], wf_ref[0], preferred_element_type=jnp.float32)
+    yb = jnp.dot(xs_ref[g, 0:640, 128:384], wb_ref[0], preferred_element_type=jnp.float32)
+    for a in (1, 2):
+        yf += jnp.dot(
+            xs_ref[g, 80 * a : 80 * a + 640, 0:256], wf_ref[a], preferred_element_type=jnp.float32
+        )
+        yb += jnp.dot(
+            xs_ref[g, 80 * a : 80 * a + 640, 128:384], wb_ref[a], preferred_element_type=jnp.float32
+        )
+    yf, yb = yf.reshape(8, 10, 8, 256), yb.reshape(8, 10, 8, 256)
+    half = low_lanes((8, 8, 8, 128))
+    swapped = jnp.where(half, yb[:, 1:9, :, 0:128], yf[:, 1:9, :, 0:128])
+    total = jnp.where(half, yf[:, 0:8, :, 0:128], yb[:, 0:8, :, 0:128])
+    total += yf[:, 2:10, :, 128:256] + yb[:, 2:10, :, 128:256]
+    total = total.reshape(512, 128) + pltpu.roll(swapped.reshape(512, 128), 64, 1)
+    total = jnp.where(g < live_ref[0], total, 0.0)
+    flat = jnp.transpose(total).astype(jnp.bfloat16)
+    out_ref[g] = flat[0:64]
+    gf_ref[g] = flat[64:128]
+
+
 def conv_kernel(
-    slots, nb_ref, live_ref, t_ref, recv_ref, wf_ref, wb_ref,
-    out_ref, gf_ref, dw_ref, pad, under, over, xs, acc,
+    slots, nb_ref, t_ref, recv_ref, xs_ref, dw_ref, pad, under, over, acc,
 ):
+    xs = xs_ref.at[0]
     g = pl.program_id(0)
     cap = recv_ref.shape[1]
 
@@ -145,26 +167,6 @@
     xs[:, 128:256] = high.astype(jnp.bfloat16)
     xs[:, 256:384] = jnp.where(first, pltpu.roll(low, 64, 1), mid).astype(jnp.bfloat16)
 
-    yf = jnp.dot(xs[0:640, 0:256], wf_ref[0], preferred_element_type=jnp.float32)
-    yb = jnp.dot(xs[0:640, 128:384], wb_ref[0], preferred_element_type=jnp.float32)
-    for a in (1, 2):
-        yf += jnp.dot(
-            xs[80 * a : 80 * a + 640, 0:256], wf_ref[a], preferred_element_type=jnp.float32
-        )
-        yb += jnp.dot(
-            xs[80 * a : 80 * a + 640, 128:384], wb_ref[a], preferred_element_type=jnp.float32
-        )
-    yf, yb = yf.reshape(8, 10, 8, 256), yb.reshape(8, 10, 8, 256)
-    half = low_lanes((8, 8, 8, 128))
-    swapped = jnp.where(half, yb[:, 1:9, :, 0:128], yf[:, 1:9, :, 0:128])
-    total = jnp.where(half, yf[:, 0:8, :, 0:128], yb[:, 0:8, :, 0:128])
-    total += yf[:, 2:10, :, 128:256] + yb[:, 2:10, :, 128:256]
-    total = total.reshape(512, 128) + pltpu.roll(swapped.reshape(512, 128), 64, 1)
-    total = jnp.where(g < live_ref[0], total, 0.0)
-    flat = jnp.transpose(total).astype(jnp.bfloat16)
-    out_ref[0] = flat[0:64]
-    gf_ref[0] = flat[64:128]
-
     turned = pltpu.roll(own.reshape(512, 128), 64, 1).reshape(8, 8, 8, 128)
     zero = jnp.zeros((8, 1, 8, 128), jnp.float32)
     g0 = jnp.concatenate([turned, zero, zero], axis=1)
@@ -189,9 +191,15 @@
 
 
 def sum_kernel(
-    n_rx, n_ry, scale, dw_ref, out_ref,
+    n_rx, n_ry, scale, live_ref, dw_ref, xs_ref, wf_ref, wb_ref, conv_ref, gf_ref, out_ref,
     src1, got1, src2, got2, part, whole, send_sem, sem1, sem2, sem3, sem4,
 ):
+    slots = xs_ref.shape[0]
+
+    def brick(g, carry=0):
+        apply_brick(g, live_ref, xs_ref, wf_ref, wb_ref, conv_ref, gf_ref)
+        return carry
+
     row, col = lax.axis_index("rx"), lax.axis_index("ry")
     size = dw_ref.shape[0] // n_ry
     piece = size // n_rx
@@ -216,6 +224,7 @@
         x = copy(src1.at[c], got1.at[col], 0, n, sem1.at[col], (row, c))
         x.start()
         sent.append(x)
+    lax.fori_loop(0, slots - 3, brick, 0)
     mine = dw_ref[pl.ds(pl.multiple_of(col * size, 8), size), :]
     for n, c in enumerate(reversed(cols)):
         copy(src1.at[c], got1.at[c], 0, n, sem1.at[c], (row, c)).wait_recv()
@@ -226,6 +235,7 @@
         x = copy(src2.at[r], got2.at[row], 1, n, sem2.at[row], (r, col))
         x.start()
         sent.append(x)
+    brick(slots - 3)
     small = src2[row]
     for n, r in enumerate(reversed(rows)):
         copy(src2.at[r], got2.at[r], 1, n, sem2.at[r], (r, col)).wait_recv()
@@ -236,6 +246,7 @@
         x = copy(part.at[row], part.at[row], 2, n, sem3.at[row], (r, col))
         x.start()
         sent.append(x)
+    brick(slots - 2)
     for n, r in enumerate(reversed(rows)):
         copy(part.at[r], part.at[r], 2, n, sem3.at[r], (r, col)).wait_recv()
 
@@ -244,6 +255,7 @@
         x.start()
         sent.append(x)
     whole[col] = part[...]
+    brick(slots - 1)
     for n, c in enumerate(reversed(cols)):
         copy(part, whole.at[c], 3, n, sem4.at[c], (row, c)).wait_recv()
     full = whole[...].astype(jnp.float32).reshape(ROWS, 128)
@@ -284,36 +296,40 @@
         name="swap",
     )(live_count, send_list, features, grad_out, weights)
 
-    block = pl.BlockSpec((1, channels, 512), lambda g: (g, 0, 0))
-    output, grad_features, dw = pl.pallas_call(
+    windows, dw = pl.pallas_call(
         functools.partial(conv_kernel, slots),
         grid=(slots,),
         out_shape=(
-            jax.ShapeDtypeStruct(features.shape, bf16),
-            jax.ShapeDtypeStruct(features.shape, bf16),
+            jax.ShapeDtypeStruct((slots, 800, 384), bf16),
             jax.ShapeDtypeStruct((ROWS, 128), f32),
         ),
-        in_specs=[smem, smem, vmem, vmem, vmem, vmem],
-        out_specs=(block, block, pl.BlockSpec((ROWS, 128), lambda g: (0, 0))),
+        in_specs=[smem, vmem, vmem],
+        out_specs=(
+            pl.BlockSpec((1, 800, 384), lambda g: (g, 0, 0)),
+            pl.BlockSpec((ROWS, 128), lambda g: (0, 0)),
+        ),
         scratch_shapes=[
             pltpu.VMEM((10, 10, 8, 128), f32),
             pltpu.VMEM((10, 10, 8, 128), f32),
             pltpu.VMEM((10, 10, 8, 128), f32),
-            pltpu.VMEM((800, 384), bf16),
             pltpu.VMEM((576, 256), f32),
         ],
         name="conv",
-    )(neighbor, live_count, cells, received, forward, backward)
+    )(neighbor, cells, received)
 
     scale = (512.0 * slots * n_rx * n_ry) ** (-0.5)
     size = ROWS // n_ry
     piece = size // n_rx
     most = max(n_rx, n_ry)
-    grad_weights = pl.pallas_call(
+    output, grad_features, grad_weights = pl.pallas_call(
         functools.partial(sum_kernel, n_rx, n_ry, scale),
-        out_shape=jax.ShapeDtypeStruct((27, channels, channels), f32),
-        in_specs=[vmem],
-        out_specs=vmem,
+        out_shape=(
+            jax.ShapeDtypeStruct(features.shape, bf16),
+            jax.ShapeDtypeStruct(features.shape, bf16),
+            jax.ShapeDtypeStruct((27, channels, channels), f32),
+        ),
+        in_specs=[smem, vmem, vmem, vmem, vmem],
+        out_specs=(vmem, vmem, vmem),
         scratch_shapes=[
             pltpu.VMEM((n_ry, size, 128), f32),
             pltpu.VMEM((n_ry, size, 128), f32),
@@ -329,7 +345,7 @@
         ],
         compiler_params=pltpu.CompilerParams(collective_id=1, has_side_effects=True),
         name="total",
-    )(dw)
+    )(live_count, dw, windows, forward, backward)
     return output, grad_features, grad_weights
 
 

time: 49.6 us -> 52.7 us (1.062)
  local copies, waits for them, and re-layouts: 2.17 us -> 5.91 us
  Pallas kernels: 45.9 us -> 45.2 us
    unnamed x1 -> x3, local copies, waits for them, and re-layouts: 2.17 us -> 5.91 us
    pallas_call x1, Pallas kernels: 11.4 us -> 8.62 us  [body(): pl.pallas_call(functools.partial(conv_kernel, slots), grid=(slots,), out_...]
    pallas_call x1, Pallas kernels: 24.5 us -> 26.6 us  [body(): pl.pallas_call(functools.partial(sum_kernel, n_rx, n_ry, scale), out_shap...]
where the time goes in v2:
time: 52.7 us; the launch traced here: 52.4 us
  Pallas kernels  45.2 us (86%)
  local copies, waits for them, and re-layouts  5.91 us (11%)
  between operations  1.3 us (2%)
    pallas_call x1, Pallas kernels, body(): pl.pallas_call(functools.partial(sum_kernel, n_rx, n_ry, scale), out_shap...  26.6 us
    pallas_call x1, Pallas kernels, body(): pl.pallas_call(functools.partial(swap_kernel, n_rx, n_ry), out_shape=(jax...  10 us
    pallas_call x1, Pallas kernels, body(): pl.pallas_call(functools.partial(conv_kernel, slots), grid=(slots,), out_...  8.62 us
    unnamed x3, local copies, waits for them, and re-layouts  5.91 us

profile of v2, /device:TPU:0, one launch (start us, length us, event | category | flops | bytes accessed | tf_op | source)
XLA Modules:
  0.0 52.4 jit_solution(18356102335541286679)
XLA Ops:
  1.3 10.0 %swap.1 = (f32[8,8,8,8,128]{4,3,2,1,0:T(8,128)}, bf16[4,4,64,128]{3,2,1,0:T(8,128)(2,1)}, bf16[3,256,256]{2,1,0:T(8,128)(2,1)}, bf16[3,256,256]{2,1,0:T(8,128)(2,1)}) custom-call(s32[1]{0:T(128)S(6)} %copy.12.live_ref, s32[4,4]{1,0:T(4,128)} %list_ref.1, bf16[8,64,512]{2,1,0:T(8,128)(2,1)} %feat_ref.1, bf16[8,64,512]{2,1,0:T(8,128)(2,1)} %grad_ref.1, ...), custom_call_target="tpu_custom_call" | custom-call | tf_op jit(solution)/shard_map/swap/pallas_call | solution.py:280
  11.3 8.6 %conv.1 = (bf16[8,800,384]{2,1,0:T(8,128)(2,1)}, f32[1024,128]{1,0:T(8,128)}) custom-call(s32[8,6]{1,0:T(8,128)} %nb_ref.1, f32[8,8,8,8,128]{4,3,2,1,0:T(8,128)} %get-tuple-element.9.t_ref, bf16[4,4,64,128]{3,2,1,0:T(8,128)(2,1)} %get-tuple-element.10.recv_ref), custom_call_target="tpu_custom_call" | custom-call | tf_op jit(solution)/shard_map/conv/pallas_call | solution.py:299
  19.9 26.6 %total.1 = (bf16[8,64,512]{2,1,0:T(8,128)(2,1)}, bf16[8,64,512]{2,1,0:T(8,128)(2,1)}, f32[27,64,64]{2,1,0:T(8,128)}) custom-call(s32[1]{0:T(128)S(6)} %copy.12.live_ref, f32[1024,128]{1,0:T(8,128)} %get-tuple-element.11.dw_ref, bf16[8,800,384]{2,1,0:T(8,128)(2,1)} %get-tuple-element.12.xs_ref, bf16[3,256,256]{2,1,0:T(8,128)(2,1)} %get-tuple-element.13.wf_ref, ...), custom_call_target="tpu_custom_call" | custom-call | tf_op jit(solution)/shard_map/total/pallas_call | solution.py:324
  46.5 1.9 %copy.13 = bf16[8,64,512]{2,1,0:T(8,128)(2,1)} copy(bf16[8,64,512]{2,1,0:T(8,128)(2,1)} %get-tuple-element.18) | data formatting | bytes 1048576
  48.4 1.9 %copy.14 = bf16[8,64,512]{2,1,0:T(8,128)(2,1)} copy(bf16[8,64,512]{2,1,0:T(8,128)(2,1)} %get-tuple-element.19) | data formatting | bytes 1048576
  50.2 2.2 %copy.15 = f32[27,64,64]{2,1,0:T(8,128)} copy(f32[27,64,64]{2,1,0:T(8,128)} %get-tuple-element.20) | data formatting | bytes 884736

commit v3 on v1

--- a/solution.py
+++ b/solution.py
@@ -189,8 +189,8 @@
 
 
 def sum_kernel(
-    n_rx, n_ry, scale, dw_ref, out_ref,
-    src1, got1, src2, got2, part, whole, send_sem, sem1, sem2, sem3, sem4,
+    n_rx, n_ry, scale, dw_ref, whole,
+    src1, got1, src2, got2, part, send_sem, sem1, sem2, sem3, sem4,
 ):
     row, col = lax.axis_index("rx"), lax.axis_index("ry")
     size = dw_ref.shape[0] // n_ry
@@ -246,15 +246,18 @@
     whole[col] = part[...]
     for n, c in enumerate(reversed(cols)):
         copy(part, whole.at[c], 3, n, sem4.at[c], (row, c)).wait_recv()
-    full = whole[...].astype(jnp.float32).reshape(ROWS, 128)
+    for x in sent:
+        x.wait_send()
+
+
+def unpack_kernel(packed_ref, out_ref):
+    full = packed_ref[...].astype(jnp.float32).reshape(ROWS, 128)
     for n in range(9):
         pair = full[64 * n : 64 * n + 64]
         out_ref[3 * n] = pair[:, 0:64]
         out_ref[3 * n + 1] = pair[:, 64:128]
         at, half = 576 + 64 * (n % 5), 64 * (n // 5)
         out_ref[3 * n + 2] = full[at : at + 64, half : half + 64]
-    for x in sent:
-        x.wait_send()
 
 
 def body(features, grad_out, weights, live_count, neighbor, send_list):
@@ -309,9 +312,9 @@
     size = ROWS // n_ry
     piece = size // n_rx
     most = max(n_rx, n_ry)
-    grad_weights = pl.pallas_call(
+    packed = pl.pallas_call(
         functools.partial(sum_kernel, n_rx, n_ry, scale),
-        out_shape=jax.ShapeDtypeStruct((27, channels, channels), f32),
+        out_shape=jax.ShapeDtypeStruct((n_ry, n_rx, piece, 128), bf16),
         in_specs=[vmem],
         out_specs=vmem,
         scratch_shapes=[
@@ -320,7 +323,6 @@
             pltpu.VMEM((n_rx, piece, 128), f32),
             pltpu.VMEM((n_rx, piece, 128), f32),
             pltpu.VMEM((n_rx, piece, 128), bf16),
-            pltpu.VMEM((n_ry, n_rx, piece, 128), bf16),
             pltpu.SemaphoreType.DMA((4, most)),
             pltpu.SemaphoreType.DMA((n_ry,)),
             pltpu.SemaphoreType.DMA((n_rx,)),
@@ -330,6 +332,13 @@
         compiler_params=pltpu.CompilerParams(collective_id=1, has_side_effects=True),
         name="total",
     )(dw)
+    grad_weights = pl.pallas_call(
+        unpack_kernel,
+        out_shape=jax.ShapeDtypeStruct((27, channels, channels), f32),
+        in_specs=[vmem],
+        out_specs=vmem,
+        name="unpack",
+    )(packed)
     return output, grad_features, grad_weights
 
 

time: 49.6 us -> 49.1 us (0.990)
  local copies, waits for them, and re-layouts: 2.17 us -> 0 us
  Pallas kernels: 45.9 us -> 47.5 us
    unnamed x1 -> x0, local copies, waits for them, and re-layouts: 2.17 us -> none
    pallas_call x0 -> x1, Pallas kernels: none -> 1.99 us  [body(): pl.pallas_call(unpack_kernel, out_shape=jax.ShapeDtypeStruct((27, channel...]
where the time goes in v3:
time: 49.1 us; the launch traced here: 48.8 us
  Pallas kernels  47.5 us (97%)
  between operations  1.3 us (3%)
    pallas_call x1, Pallas kernels, body(): pl.pallas_call(functools.partial(sum_kernel, n_rx, n_ry, scale), out_shap...  24.1 us
    pallas_call x1, Pallas kernels, body(): pl.pallas_call(functools.partial(conv_kernel, slots), grid=(slots,), out_...  11.4 us
    pallas_call x1, Pallas kernels, body(): pl.pallas_call(functools.partial(swap_kernel, n_rx, n_ry), out_shape=(jax...  10 us
    pallas_call x1, Pallas kernels, body(): pl.pallas_call(unpack_kernel, out_shape=jax.ShapeDtypeStruct((27, channel...  1.99 us

profile of v3, /device:TPU:0, one launch (start us, length us, event | category | flops | bytes accessed | tf_op | source)
XLA Modules:
  0.0 48.8 jit_solution(16618813571757295619)
XLA Ops:
  1.3 10.0 %swap.1 = (f32[8,8,8,8,128]{4,3,2,1,0:T(8,128)}, bf16[4,4,64,128]{3,2,1,0:T(8,128)(2,1)}, bf16[3,256,256]{2,1,0:T(8,128)(2,1)}, bf16[3,256,256]{2,1,0:T(8,128)(2,1)}) custom-call(s32[1]{0:T(128)S(6)} %copy.9.live_ref, s32[4,4]{1,0:T(4,128)} %list_ref.1, bf16[8,64,512]{2,1,0:T(8,128)(2,1)} %feat_ref.1, bf16[8,64,512]{2,1,0:T(8,128)(2,1)} %grad_ref.1, ...), custom_call_target="tpu_custom_call" | custom-call | tf_op jit(solution)/shard_map/swap/pallas_call | solution.py:271
  11.3 11.4 %conv.1 = (bf16[8,64,512]{2,1,0:T(8,128)(2,1)}, bf16[8,64,512]{2,1,0:T(8,128)(2,1)}, f32[1024,128]{1,0:T(8,128)}) custom-call(s32[8,6]{1,0:T(8,128)} %nb_ref.1, s32[1]{0:T(128)S(6)} %copy.9.live_ref, f32[8,8,8,8,128]{4,3,2,1,0:T(8,128)} %get-tuple-element.10.t_ref, bf16[4,4,64,128]{3,2,1,0:T(8,128)(2,1)} %get-tuple-element.11.recv_ref, ...), custom_call_target="tpu_custom_call" | custom-call | tf_op jit(solution)/shard_map/conv/pallas_call | solution.py:291
  22.7 24.1 %total.1.packed_ref = bf16[8,4,32,128]{3,2,1,0:T(8,128)(2,1)} custom-call(f32[1024,128]{1,0:T(8,128)} %get-tuple-element.16.dw_ref), custom_call_target="tpu_custom_call" | custom-call | tf_op jit(solution)/shard_map/total/pallas_call | solution.py:315
  46.8 2.0 %unpack.1 = f32[27,64,64]{2,1,0:T(8,128)} custom-call(bf16[8,4,32,128]{3,2,1,0:T(8,128)(2,1)} %total.1.packed_ref), custom_call_target="tpu_custom_call" | custom-call | tf_op jit(solution)/shard_map/unpack/pallas_call | solution.py:335
